TPU v7x, 32 devices: a whole 2x2x4 slice. The times are simulated.
32 devices in a mesh: grp: 2 (over x), gx: 16 (over z, y, core).
Axes of the slice: x: 2, y: 2, z: 4, core: 2. Of those that a mesh axis runs over, the one named last changes fastest.
Arguments:
- grain_ids: int32 [96, 32, 512], P(('grp', 'gx')), parts along dimension 0, may hold values from 0 to 7
- jitter: bfloat16 [8, 96, 32, 512], P(None, ('grp', 'gx')), parts along dimension 1, may hold values from 0 to 0.5
- class_table: int32 [8, 8], replicated, may hold values from 0 to 3
- chosen: int32 [2], replicated, may hold values from 0 to 7
Outputs:
- order_params: float32 [8, 96, 32, 512], P(None, ('grp', 'gx')), parts along dimension 1
- correlation: float32 [2, 96, 32, 512], P(None, ('grp', 'gx')), parts along dimension 1
There are 2 independent parts, one for each index of `grp`. A program takes and returns all parts, laid end to end along the dimension named above; an argument that names none is the same for every part. Nothing has to cross between parts.
All inputs are finite; a program needn't handle non-finite values.
Results may differ from a plain program's by a relative error of at most 0.0003.
Values sent between devices are 32-bit elements; how exact they have to be, the bound alone decides.
No kernel may reach another device: no remote copies, remote signals or barrier semaphores. Data moves between devices by JAX's collectives and lax.ppermute only.
A program may use at most 128 MiB of HBM per device.

v0:
```python
import math
import jax
import jax.numpy as jnp
from jax import lax
from jax.sharding import PartitionSpec as P

STEPS = 3
HIGH = lax.Precision.HIGHEST


def with_halo(value, sides, width):
    for axis, dim in sides:
        peers, length = (lax.axis_size(axis), value.shape[dim])
        up = [(i, (i + 1) % peers) for i in range(peers)]
        down = [(j, i) for i, j in up]
        last = lax.slice_in_dim(value, length - width, length, axis=dim)
        initial = lax.slice_in_dim(value, 0, width, axis=dim)
        before = lax.ppermute(last, axis, up)
        after = lax.ppermute(initial, axis, down)
        value = jnp.concatenate([before, value, after], axis=dim)
    return value


def tables(length):
    index = lax.iota(jnp.int32, length)
    product = index[:, None] * index[None, :] % length
    angle = product.astype(jnp.float32) * (2.0 * math.pi / length)
    return (jnp.cos(angle), jnp.sin(angle))


def onehot_of(grain_ids):
    return (grain_ids[None] == lax.iota(jnp.int32, 8)[:, None, None, None]).astype(jnp.float32)


def levels_map(onehot, class_table):
    levels = 0.4 + 0.2 * class_table.astype(jnp.float32)
    return jnp.einsum("gi,gxzy->ixzy", levels, onehot, precision=HIGH)


def advance(extended, mobility):
    center = extended[:, 1:-1]
    lap = extended[:, 2:] + extended[:, :-2]
    lap = lap + jnp.roll(center, -1, 2) + jnp.roll(center, 1, 2)
    lap = lap + jnp.roll(center, -1, 3) + jnp.roll(center, 1, 3)
    lap = lap - 6.0 * center
    total = jnp.sum(center * center, axis=0)
    drive = -center + center * center * center + 3.0 * center * (total[None] - center * center)
    return center - 0.12 * mobility * (drive - lap)


def forward_planes(fields, cos_y, sin_y, cos_z, sin_z):
    real_y = jnp.dot(fields, cos_y, precision=HIGH)
    imag_y = -jnp.dot(fields, sin_y, precision=HIGH)
    real_z = jnp.einsum("kz,fxzy->fxky", cos_z, real_y, precision=HIGH) + jnp.einsum(
        "kz,fxzy->fxky", sin_z, imag_y, precision=HIGH
    )
    imag_z = jnp.einsum("kz,fxzy->fxky", cos_z, imag_y, precision=HIGH) - jnp.einsum(
        "kz,fxzy->fxky", sin_z, real_y, precision=HIGH
    )
    planes = fields.shape[1]
    return (
        real_z.reshape(fields.shape[0], planes, -1),
        imag_z.reshape(fields.shape[0], planes, -1),
    )


def line_power(real_part, imag_part, cos_x, sin_x, offset):
    real_x = jnp.einsum("kx,fxc->fkc", cos_x, real_part, precision=HIGH) + jnp.einsum(
        "kx,fxc->fkc", sin_x, imag_part, precision=HIGH
    )
    imag_x = jnp.einsum("kx,fxc->fkc", cos_x, imag_part, precision=HIGH) - jnp.einsum(
        "kx,fxc->fkc", sin_x, real_part, precision=HIGH
    )
    power = real_x * real_x + imag_x * imag_x
    freq_x = lax.iota(jnp.int32, power.shape[1])[:, None]
    column = offset + lax.iota(jnp.int32, power.shape[2])[None, :]
    keep = jnp.logical_not(jnp.logical_and(freq_x == 0, column == 0))
    power = power * keep.astype(jnp.float32)[None]
    back_real = jnp.einsum("kx,fkc->fxc", cos_x, power, precision=HIGH)
    back_imag = jnp.einsum("kx,fkc->fxc", sin_x, power, precision=HIGH)
    return (back_real, back_imag)


def inverse_planes(back_real, back_imag, cos_y, sin_y, cos_z, sin_z, depth, width, count):
    fields = back_real.shape[0]
    planes = back_real.shape[1]
    back_real = back_real.reshape(fields, planes, depth, width)
    back_imag = back_imag.reshape(fields, planes, depth, width)
    real_z = jnp.einsum("kz,fxky->fxzy", cos_z, back_real, precision=HIGH) - jnp.einsum(
        "kz,fxky->fxzy", sin_z, back_imag, precision=HIGH
    )
    imag_z = jnp.einsum("kz,fxky->fxzy", cos_z, back_imag, precision=HIGH) + jnp.einsum(
        "kz,fxky->fxzy", sin_z, back_real, precision=HIGH
    )
    result = jnp.dot(real_z, cos_y, precision=HIGH) - jnp.dot(imag_z, sin_y, precision=HIGH)
    return result / (count * count)


def shards(grain_ids, jitter, class_table, chosen):
    planes = grain_ids.shape[0]
    depth = grain_ids.shape[1]
    width = grain_ids.shape[2]
    devices = lax.axis_size("gx")
    onehot = onehot_of(grain_ids)
    eta = 0.6 * onehot + jitter.astype(jnp.float32)
    mobility = levels_map(onehot, class_table)
    for step in range(STEPS):
        extended = with_halo(eta, (("gx", 1),), 1)
        eta = advance(extended, mobility)
    select = (chosen[:, None] == lax.iota(jnp.int32, 8)[None, :]).astype(jnp.float32)
    fields = jnp.einsum("ki,ixzy->kxzy", select, eta, precision=HIGH)
    cos_y, sin_y = tables(width)
    cos_z, sin_z = tables(depth)
    total_x = planes * devices
    cos_x, sin_x = tables(total_x)
    count = float(total_x * depth * width)
    columns = depth * width // devices
    offset = lax.axis_index("gx") * columns
    real_part, imag_part = forward_planes(fields, cos_y, sin_y, cos_z, sin_z)
    stacked = jnp.concatenate([real_part, imag_part], axis=0)
    lines = lax.all_to_all(stacked, "gx", split_axis=2, concat_axis=1, tiled=True)
    back_real, back_imag = line_power(lines[:2], lines[2:], cos_x, sin_x, offset)
    returned = lax.all_to_all(
        jnp.concatenate([back_real, back_imag], axis=0),
        "gx",
        split_axis=1,
        concat_axis=2,
        tiled=True,
    )
    correlation = inverse_planes(
        returned[:2], returned[2:], cos_y, sin_y, cos_z, sin_z, depth, width, count
    )
    return (eta, correlation)


def solution(mesh):
    in_specs = (P(("grp", "gx"), None, None), P(None, ("grp", "gx"), None, None), P(), P())
    out_specs = (P(None, ("grp", "gx"), None, None), P(None, ("grp", "gx"), None, None))
    return jax.shard_map(shards, mesh=mesh, in_specs=in_specs, out_specs=out_specs, check_vma=False)
```

profile of v0, /device:TPU:11, one launch (start us, length us, event | category | flops | bytes accessed | tf_op | source)
XLA Modules:
  0.0 307.3 jit_solution(3220175203014402098)
XLA Ops:
  0.6 1.8 convert_add_fusion
  2.5 0.7 collective-permute-start
  3.3 1.2 collective-permute-start.1
  4.5 0.4 fusion.241
  4.9 0.2 fusion.238
  5.1 14.7 %multiply_subtract_fusion.2 = f32[8,3,32,512]{3,0,2,1:T(8,128)S(1)} fusion(bf16[8,3,32,512]{3,2,1,0:T(8,128)(2,1)S(1)} %copy-done.1, s32[3,32,512]{2,1,0:T(8,128)S(1)} %copy-done), kind=kOutput, calls=%fused_computation.12 | output fusion | flops 4374535 | bytes 2555904 | tf_op jit(solution)/shard_map/sub | solution.py:47
  19.9 0.6 fusion.239
  20.5 0.1 copy-done.2
  20.6 2.2 fusion.16
  22.8 0.4 fusion.236
  23.2 0.1 fusion.237
  23.3 0.2 fusion.233
  23.5 0.2 collective-permute-start.2
  23.7 1.6 collective-permute-start.3
  25.3 0.6 fusion.234
  25.9 11.9 %collective-permute-done.2 = f32[8,1,32,512]{3,0,2,1:T(8,128)S(1)} collective-permute-done((f32[8,1,32,512]{3,0,2,1:T(8,128)S(1)}, f32[8,1,32,512]{3,0,2,1:T(8,128)S(1)}, u32[]{:S(2)}, u32[]{:S(2)}) %collective-permute-start.2) | collective-permute-done | bytes 524320 | tf_op jit(solution)/shard_map/ppermute | solution.py:19
  37.8 34.6 %fusion.21 = f32[8,3,32,512]{3,0,2,1:T(8,128)S(1)} fusion(f32[8,3,32,512]{3,0,2,1:T(8,128)S(1)} %get-tuple-element.42, f32[8,3,32,512]{3,0,2,1:T(8,128)S(1)} %get-tuple-element.43, f32[8,1,32,512]{3,0,2,1:T(8,128)S(1)} %collective-permute-done.3, f32[8,1,32,512]{3,0,2,1:T(8,128)S(1)} %collective-permute-done.2, f32[8,3,1,512]{3,0,2,1:T(8,128)S(1)} %get-tuple-element.23, ...), kind=kOutput, calls=%fused_computation.24 | output fusion | flops 9879559 | bytes 12058624 | tf_op jit(solution)/shard_map/sub | solution.py:47
  72.4 0.4 fusion.231
  72.9 0.2 fusion.228
  73.2 2.3 collective-permute-start.5
  75.4 0.6 fusion.229
  76.0 11.4 %collective-permute-done.4 = f32[8,1,32,512]{3,0,2,1:T(8,128)S(1)} collective-permute-done((f32[8,1,32,512]{3,0,2,1:T(8,128)S(1)}, f32[8,1,32,512]{3,0,2,1:T(8,128)S(1)}, u32[]{:S(2)}, u32[]{:S(2)}) %collective-permute-start.4) | collective-permute-done | bytes 524320 | tf_op jit(solution)/shard_map/ppermute | solution.py:19
  87.4 34.6 %fusion.26 = f32[8,3,32,512]{3,0,2,1:T(8,128)S(1)} fusion(f32[8,3,32,512]{3,0,2,1:T(8,128)S(1)} %fusion.21, f32[8,3,32,512]{3,0,2,1:T(8,128)S(1)} %get-tuple-element.43, f32[8,1,32,512]{3,0,2,1:T(8,128)S(1)} %collective-permute-done.5, f32[8,1,32,512]{3,0,2,1:T(8,128)S(1)} %collective-permute-done.4, f32[8,3,1,512]{3,0,2,1:T(8,128)S(1)} %get-tuple-element.13, ...), kind=kOutput, calls=%fused_computation.29 | output fusion | flops 9879559 | bytes 12058624 | tf_op jit(solution)/shard_map/sub | solution.py:47
  122.1 0.9 fusion.155
  122.9 5.1 %fusion.62 = f32[2,3,32,512]{3,2,1,0:T(8,128)S(1)} fusion(f32[2,3,32,512]{3,0,2,1:T(2,128)S(1)} %fusion.155), kind=kOutput, calls=%fused_computation.86 | convolution fusion | flops 607649792 | bytes 786432 | tf_op jit(solution)/shard_map/dot_general | solution.py:52
  128.1 5.1 %convolution_negate_fusion = f32[2,3,32,512]{3,2,1,0:T(8,128)S(1)} fusion(f32[2,3,32,512]{3,0,2,1:T(2,128)S(1)} %fusion.155), kind=kOutput, calls=%fused_computation.76 | convolution fusion | flops 607748096 | bytes 786432 | tf_op jit(solution)/shard_map/dot_general | solution.py:53
  133.2 0.6 fusion.116
  133.8 0.6 fusion.114
  134.4 0.6 fusion.52
  135.0 0.3 reshape.68
  135.3 0.6 fusion.51
  136.0 0.3 reshape.69
  136.3 0.4 pad_maximum_fusion.6
  136.7 20.3 %copy.46 = f32[4,3,16384]{0,1,2:T(4,128)} copy(f32[4,3,16384]{2,0,1:T(4,128)S(1)} %pad_maximum_fusion.6) | data formatting | bytes 1572864 | tf_op jit(solution)/shard_map/concatenate | solution.py:120
  157.0 24.8 %reshape.88 = f32[16,1,12288]{2,1,0:T(1,128)} reshape(f32[16384,3,4]{2,1,0:T(4,128)} %bitcast.118) | data formatting | bytes 1572864
  181.8 7.3 %all-to-all-start = ((f32[16,1,12288]{2,1,0:T(1,128)}), f32[16,1,12288]{2,1,0:T(1,128)S(1)}, u32[]{:S(2)}, u32[]{:S(2)}) async-start(f32[16,1,12288]{2,1,0:T(1,128)} %reshape.88), calls=%async_computation | async-start | bytes 1572864 | tf_op jit(solution)/shard_map/all_to_all | solution.py:121
  189.2 0.1 not_convert_fusion
  189.3 19.3 %all-to-all-done = f32[16,1,12288]{2,1,0:T(1,128)S(1)} async-done(((f32[16,1,12288]{2,1,0:T(1,128)}), f32[16,1,12288]{2,1,0:T(1,128)S(1)}, u32[]{:S(2)}, u32[]{:S(2)}) %all-to-all-start) | async-done | bytes 786464 | tf_op jit(solution)/shard_map/all_to_all | solution.py:121
  208.6 0.5 broadcast.133
  209.1 2.5 reduce
  211.6 33.0 %reshape.89 = f32[16384,3,4]{2,1,0:T(4,128)} reshape(f32[16,12288]{1,0:T(8,128)S(1)} %reduce) | data formatting | bytes 1572864
  244.7 18.5 %copy.81 = f32[4,3,16,1024]{3,2,0,1:T(8,128)S(1)} copy(f32[4,3,16,1024]{0,1,3,2:T(4,128)} %bitcast.119) | data formatting | bytes 1572864 | tf_op jit(solution)/shard_map/all_to_all | solution.py:121
  263.2 0.1 fusion.244
  263.2 0.3 copy.51
  263.6 0.7 fusion.76
  264.2 0.3 copy.48
  264.6 0.7 fusion.80
  265.2 0.7 fusion.49
  265.9 0.7 fusion.55
  266.7 0.6 convolution_bitcast_fusion
  267.2 0.6 convolution_bitcast_fusion.1
  267.9 1.4 copy.58
  269.3 4.6 %all-to-all-start.1 = ((f32[4,48,1024]{2,0,1:T(4,128)}), f32[4,48,1024]{2,0,1:T(4,128)S(1)}, u32[]{:S(2)}, u32[]{:S(2)}) async-start(f32[4,48,1024]{2,0,1:T(4,128)} %copy.58), calls=%async_computation.1 | async-start | bytes 1572864 | tf_op jit(solution)/shard_map/all_to_all | solution.py:123
  273.9 2.1 copy.61
  276.0 17.5 %all-to-all-done.1 = f32[4,48,1024]{2,0,1:T(4,128)S(1)} async-done(((f32[4,48,1024]{2,0,1:T(4,128)}), f32[4,48,1024]{2,0,1:T(4,128)S(1)}, u32[]{:S(2)}, u32[]{:S(2)}) %all-to-all-start.1) | async-done | bytes 786464 | tf_op jit(solution)/shard_map/all_to_all | solution.py:123
  293.5 0.3 fusion.243
  293.8 0.1 copy.60
  294.0 0.5 fusion.110
  294.6 0.1 copy.59
  294.8 0.5 fusion.112
  295.3 0.6 fusion.47
  295.9 0.6 fusion.48
  296.4 5.1 %fusion.60 = f32[2,3,32,512]{3,2,1,0:T(8,128)S(1)} fusion(f32[2,3,32,512]{3,2,1,0:T(8,128)S(1)} %fusion.48), kind=kOutput, calls=%fused_computation.84 | convolution fusion | flops 607649792 | bytes 786432 | tf_op jit(solution)/shard_map/dot_general | solution.py:95
  301.5 5.6 %fusion.56 = f32[2,3,32,512]{3,2,1,0:T(8,128)} fusion(f32[2,3,32,512]{3,2,1,0:T(8,128)S(1)} %fusion.60, f32[2,3,32,512]{3,2,1,0:T(8,128)S(1)} %fusion.47), kind=kOutput, calls=%fused_computation.80 | convolution fusion | flops 607846400 | bytes 1179648 | tf_op jit(solution)/shard_map/dot_general | solution.py:95
  (24 shorter events, 0.5 us)
Async XLA Ops:
  2.5 17.9 %collective-permute-start = (f32[8,1,32,512]{3,0,2,1:T(8,128)S(1)}, f32[8,1,32,512]{3,0,2,1:T(8,128)S(1)}, u32[]{:S(2)}, u32[]{:S(2)}) collective-permute-start(f32[8,1,32,512]{3,0,2,1:T(8,128)S(1)} %get-tuple-element.36), channel_id=1, source_target_pairs={{1,0},{2,1},{3,2},{4,3},{5,4},{6,5},{7,6},{8,7},{9,8},{10,9},{11,1... | collective-permute-start | bytes 1572872 | tf_op jit(solution)/shard_map/ppermute | solution.py:19
  3.2 1.8 copy-start
  3.2 1.8 copy-start.1
  3.3 17.2 %collective-permute-start.1 = (f32[8,1,32,512]{3,0,2,1:T(8,128)S(1)}, f32[8,1,32,512]{3,0,2,1:T(8,128)S(1)}, u32[]{:S(2)}, u32[]{:S(2)}) collective-permute-start(f32[8,1,32,512]{3,0,2,1:T(8,128)S(1)} %get-tuple-element.37), channel_id=1, source_target_pairs={{0,1},{1,2},{2,3},{3,4},{4,5},{5,6},{6,7},{7,8},{8,9},{9,10},{10,1... | collective-permute-start | bytes 1572872 | tf_op jit(solution)/shard_map/ppermute | solution.py:18
  19.9 0.7 copy-start.2
  23.5 14.3 %collective-permute-start.2 = (f32[8,1,32,512]{3,0,2,1:T(8,128)S(1)}, f32[8,1,32,512]{3,0,2,1:T(8,128)S(1)}, u32[]{:S(2)}, u32[]{:S(2)}) collective-permute-start(f32[8,1,32,512]{3,0,2,1:T(8,128)S(1)} %get-tuple-element.26), channel_id=1, source_target_pairs={{1,0},{2,1},{3,2},{4,3},{5,4},{6,5},{7,6},{8,7},{9,8},{10,9},{11,1... | collective-permute-start | bytes 1572872 | tf_op jit(solution)/shard_map/ppermute | solution.py:19
  23.7 14.1 %collective-permute-start.3 = (f32[8,1,32,512]{3,0,2,1:T(8,128)S(1)}, f32[8,1,32,512]{3,0,2,1:T(8,128)S(1)}, u32[]{:S(2)}, u32[]{:S(2)}) collective-permute-start(f32[8,1,32,512]{3,0,2,1:T(8,128)S(1)} %get-tuple-element.27), channel_id=1, source_target_pairs={{0,1},{1,2},{2,3},{3,4},{4,5},{5,6},{6,7},{7,8},{8,9},{9,10},{10,1... | collective-permute-start | bytes 1572872 | tf_op jit(solution)/shard_map/ppermute | solution.py:18
  73.1 14.3 %collective-permute-start.4 = (f32[8,1,32,512]{3,0,2,1:T(8,128)S(1)}, f32[8,1,32,512]{3,0,2,1:T(8,128)S(1)}, u32[]{:S(2)}, u32[]{:S(2)}) collective-permute-start(f32[8,1,32,512]{3,0,2,1:T(8,128)S(1)} %get-tuple-element.16), channel_id=1, source_target_pairs={{1,0},{2,1},{3,2},{4,3},{5,4},{6,5},{7,6},{8,7},{9,8},{10,9},{11,1... | collective-permute-start | bytes 1572872 | tf_op jit(solution)/shard_map/ppermute | solution.py:19
  73.2 14.2 %collective-permute-start.5 = (f32[8,1,32,512]{3,0,2,1:T(8,128)S(1)}, f32[8,1,32,512]{3,0,2,1:T(8,128)S(1)}, u32[]{:S(2)}, u32[]{:S(2)}) collective-permute-start(f32[8,1,32,512]{3,0,2,1:T(8,128)S(1)} %get-tuple-element.17), channel_id=1, source_target_pairs={{0,1},{1,2},{2,3},{3,4},{4,5},{5,6},{6,7},{7,8},{8,9},{9,10},{10,1... | collective-permute-start | bytes 1572872 | tf_op jit(solution)/shard_map/ppermute | solution.py:18
  87.4 34.7 %copy-start.3 = (s32[2]{0:T(128)S(1)}, s32[2]{0:T(128)}, u32[]{:S(2)}) copy-start(s32[2]{0:T(128)} %param.7) | copy-start | bytes 28
  181.8 26.8 %all-to-all-start = ((f32[16,1,12288]{2,1,0:T(1,128)}), f32[16,1,12288]{2,1,0:T(1,128)S(1)}, u32[]{:S(2)}, u32[]{:S(2)}) async-start(f32[16,1,12288]{2,1,0:T(1,128)} %reshape.88), calls=%async_computation | async-start | bytes 1572864 | tf_op jit(solution)/shard_map/all_to_all | solution.py:121
  269.3 24.2 %all-to-all-start.1 = ((f32[4,48,1024]{2,0,1:T(4,128)}), f32[4,48,1024]{2,0,1:T(4,128)S(1)}, u32[]{:S(2)}, u32[]{:S(2)}) async-start(f32[4,48,1024]{2,0,1:T(4,128)} %copy.58), calls=%async_computation.1 | async-start | bytes 1572864 | tf_op jit(solution)/shard_map/all_to_all | solution.py:123
where the time goes:
time: 313 us; the launch traced here: 307 us
  local copies, waits for them, and re-layouts  107 us (34%)
  other arithmetic  88.9 us (28%)
  waiting for transfers between devices  60.1 us (19%)
  matrix products  32.5 us (10%)
  starting transfers between devices  18 us (6%)
    sub x3, other arithmetic, advance(): total[None] - center * center  84 us
    unnamed x11, local copies, waits for them, and re-layouts  60 us
    ppermute x3, waiting for transfers between devices, with_halo(): after = lax.ppermute(initial, axis, down)  23.3 us
    concatenate x1, local copies, waits for them, and re-layouts, shards(): stacked = jnp.concatenate([real_part, imag_part], axis=0)  20.3 us
    all_to_all x1, waiting for transfers between devices, shards(): lax.all_to_all(stacked, 'gx', split_axis=2, concat_axis=1, tiled=True)  19.3 us
    all_to_all x2, local copies, waits for them, and re-layouts, shards(): lax.all_to_all(stacked, 'gx', split_axis=2, concat_axis=1, tiled=True)  19 us
    all_to_all x1, waiting for transfers between devices, shards(): lax.all_to_all(jnp.concatenate([back_real, back_imag], axis=0), 'gx', spl...  17.5 us
    all_to_all x1, starting transfers between devices, shards(): lax.all_to_all(stacked, 'gx', split_axis=2, concat_axis=1, tiled=True)  7.34 us
  transfers between devices with their start and end apart: 8, of which 4 were waited for; matrix products, arithmetic and copies ran while one was open for 6% of the time, Pallas kernels for 0%

commit v1 on v0

--- a/solution.py
+++ b/solution.py
@@ -3,6 +3,7 @@
 import jax.numpy as jnp
 from jax import lax
 from jax.sharding import PartitionSpec as P
+from jax.lax import axis_index, axis_size, ppermute
 
 STEPS = 3
 HIGH = lax.Precision.HIGHEST
@@ -118,7 +119,22 @@
     offset = lax.axis_index("gx") * columns
     real_part, imag_part = forward_planes(fields, cos_y, sin_y, cos_z, sin_z)
     stacked = jnp.concatenate([real_part, imag_part], axis=0)
-    lines = lax.all_to_all(stacked, "gx", split_axis=2, concat_axis=1, tiled=True)
+    row_out = axis_size("gx")
+    top = axis_index("gx")
+    built, formed = (row_out, top)
+    newest = stacked.shape[2] // built
+    w2 = list(stacked.shape)
+    w2[2] = newest
+    plain = w2[1]
+    w2[1] = plain * built
+    lines = jnp.zeros(w2, stacked.dtype)
+    m = 0
+    while m < built:
+        w_next = lax.dynamic_slice_in_dim(stacked, (formed ^ m) * newest, newest, axis=2)
+        if m:
+            w_next = ppermute(w_next, "gx", [(w, w ^ m) for w in range(built)])
+        lines = lax.dynamic_update_slice_in_dim(lines, w_next, (formed ^ m) * plain, axis=1)
+        m += 1
     back_real, back_imag = line_power(lines[:2], lines[2:], cos_x, sin_x, offset)
     returned = lax.all_to_all(
         jnp.concatenate([back_real, back_imag], axis=0),

time: 313 us -> 216 us (0.69); the launches traced: 307 us -> 215 us
  local copies, waits for them, and re-layouts: 107 us -> 23.1 us
  other arithmetic: 88.9 us -> 73.2 us
  starting transfers between devices: 18 us -> 33.3 us
  waiting for transfers between devices: 60.1 us -> 49.2 us
    unnamed x11 -> x20, local copies, waits for them, and re-layouts: 60 us -> 2.7 us
    ppermute x0 -> x15, starting transfers between devices: none -> 20.8 us  [shards(): w_next = ppermute(w_next, 'gx', [(w, w ^ m) for w in range(built)])]
    concatenate x1, local copies, waits for them, and re-layouts: 20.3 us -> 0.13 us  [shards(): stacked = jnp.concatenate([real_part, imag_part], axis=0)]
    all_to_all x1 -> x0, waiting for transfers between devices: 19.3 us -> none  [shards(): lax.all_to_all(stacked, 'gx', split_axis=2, concat_axis=1, tiled=True)]
    all_to_all x2 -> x0, local copies, waits for them, and re-layouts: 19 us -> none  [shards(): lax.all_to_all(stacked, 'gx', split_axis=2, concat_axis=1, tiled=True)]
    sub x3, other arithmetic: 84 us -> 71.2 us  [advance(): total[None] - center * center]
    dynamic_update_slice x0 -> x16, local copies, waits for them, and re-layouts: none -> 10.6 us  [shards(): lax.dynamic_update_slice_in_dim(lines, w_next, (formed ^ m) * plain, axis=1)]
    all_to_all x1 -> x0, starting transfers between devices: 7.34 us -> none  [shards(): lax.all_to_all(stacked, 'gx', split_axis=2, concat_axis=1, tiled=True)]
  transfers between devices with their start and end apart: 8 -> 22, of which waited for: 4 -> 7; matrix products, arithmetic and copies ran while one was open for 6% -> 8% of each run, Pallas kernels for 0% -> 0%
where the time goes in v1:
time: 216 us; the launch traced here: 215 us
  other arithmetic  73.2 us (34%)
  waiting for transfers between devices  49.2 us (23%)
  matrix products  35.2 us (16%)
  starting transfers between devices  33.3 us (15%)
  local copies, waits for them, and re-layouts  23.1 us (11%)
    sub x3, other arithmetic, advance(): total[None] - center * center  71.2 us
    ppermute x3, waiting for transfers between devices, with_halo(): after = lax.ppermute(initial, axis, down)  28.8 us
    ppermute x15, starting transfers between devices, shards(): w_next = ppermute(w_next, 'gx', [(w, w ^ m) for w in range(built)])  20.8 us
    all_to_all x1, waiting for transfers between devices, shards(): lax.all_to_all(jnp.concatenate([back_real, back_imag], axis=0), 'gx', spl...  17.5 us
    dynamic_update_slice x16, local copies, waits for them, and re-layouts, shards(): lax.dynamic_update_slice_in_dim(lines, w_next, (formed ^ m) * plain, axis=1)  10.6 us
    all_to_all x1, starting transfers between devices, shards(): lax.all_to_all(jnp.concatenate([back_real, back_imag], axis=0), 'gx', spl...  7.1 us
    dot_general x1, matrix products, inverse_planes(): jnp.dot(imag_z, sin_y, precision=HIGH)  5.6 us
    dot_general x1, matrix products, forward_planes(): real_y = jnp.dot(fields, cos_y, precision=HIGH)  5.12 us
  transfers between devices with their start and end apart: 22, of which 7 were waited for; matrix products, arithmetic and copies ran while one was open for 8% of the time, Pallas kernels for 0%

profile of v1, /device:TPU:11, one launch (start us, length us, event | category | flops | bytes accessed | tf_op | source)
XLA Modules:
  0.0 215.2 jit_solution(718094998113069227)
XLA Ops:
  0.6 1.8 convert_add_fusion
  2.4 1.1 fusion.238
  3.5 0.7 collective-permute-start
  4.2 1.1 collective-permute-start.1
  5.3 1.6 fusion.237
  6.9 0.9 fusion.234
  7.8 0.5 copy-done.5
  8.3 1.9 multiply_subtract_fusion.2
  10.3 0.5 fusion.235
  10.8 7.3 %collective-permute-done = f32[8,1,32,512]{3,0,2,1:T(8,128)} collective-permute-done((f32[8,1,32,512]{3,0,2,1:T(8,128)}, f32[8,1,32,512]{3,0,2,1:T(8,128)}, u32[]{:S(2)}, u32[]{:S(2)}) %collective-permute-start) | collective-permute-done | bytes 524320 | tf_op jit(solution)/shard_map/ppermute | solution.py:20
  18.1 3.4 %fusion.16 = (f32[8,3,32,512]{3,0,2,1:T(8,128)S(1)}, f32[8,3,32,512]{3,0,2,1:T(8,128)S(1)}) fusion(f32[8,3,32,512]{3,0,2,1:T(8,128)S(1)} %convert_add_fusion, f32[8,1,32,512]{3,0,2,1:T(8,128)} %collective-permute-done.1, f32[8,1,32,512]{3,0,2,1:T(8,128)} %collective-permute-done, f32[8,3,1,512]{3,0,2,1:T(8,128)S(1)} %get-tuple-element.33, ...), kind=kOutput, calls=%fused_computation.19 | convolution fusion | flops 47579328 | bytes 13828352 | tf_op jit(solution)/shard_map/gi,gxzy->ixzy/dot_general | solution.py:38
  21.5 0.4 fusion.232
  22.3 1.8 collective-permute-start.3
  24.1 0.6 fusion.230
  24.7 11.5 %collective-permute-done.2 = f32[8,1,32,512]{3,0,2,1:T(8,128)S(1)} collective-permute-done((f32[8,1,32,512]{3,0,2,1:T(8,128)S(1)}, f32[8,1,32,512]{3,0,2,1:T(8,128)S(1)}, u32[]{:S(2)}, u32[]{:S(2)}) %collective-permute-start.2) | collective-permute-done | bytes 524320 | tf_op jit(solution)/shard_map/ppermute | solution.py:20
  36.2 34.6 %fusion.21 = f32[8,3,32,512]{3,0,2,1:T(8,128)S(1)} fusion(f32[8,3,32,512]{3,0,2,1:T(8,128)S(1)} %get-tuple-element.56, f32[8,3,32,512]{3,0,2,1:T(8,128)S(1)} %get-tuple-element.57, f32[8,1,32,512]{3,0,2,1:T(8,128)S(1)} %collective-permute-done.3, f32[8,1,32,512]{3,0,2,1:T(8,128)S(1)} %collective-permute-done.2, f32[8,3,1,512]{3,0,2,1:T(8,128)S(1)} %get-tuple-element.23, ...), kind=kOutput, calls=%fused_computation.24 | output fusion | flops 9879559 | bytes 12058624 | tf_op jit(solution)/shard_map/sub | solution.py:48
  71.6 1.7 collective-permute-start.5
  73.3 0.6 fusion.225
  73.9 10.0 %collective-permute-done.4 = f32[8,1,32,512]{3,0,2,1:T(8,128)S(1)} collective-permute-done((f32[8,1,32,512]{3,0,2,1:T(8,128)S(1)}, f32[8,1,32,512]{3,0,2,1:T(8,128)S(1)}, u32[]{:S(2)}, u32[]{:S(2)}) %collective-permute-start.4) | collective-permute-done | bytes 524320 | tf_op jit(solution)/shard_map/ppermute | solution.py:20
  83.9 34.6 %fusion.26 = f32[8,3,32,512]{3,0,2,1:T(8,128)S(1)} fusion(f32[8,3,32,512]{3,0,2,1:T(8,128)S(1)} %fusion.21, f32[8,3,32,512]{3,0,2,1:T(8,128)S(1)} %get-tuple-element.57, f32[8,1,32,512]{3,0,2,1:T(8,128)S(1)} %collective-permute-done.5, f32[8,1,32,512]{3,0,2,1:T(8,128)S(1)} %collective-permute-done.4, f32[8,3,1,512]{3,0,2,1:T(8,128)S(1)} %get-tuple-element.13, ...), kind=kOutput, calls=%fused_computation.29 | output fusion | flops 9879559 | bytes 12058624 | tf_op jit(solution)/shard_map/sub | solution.py:48
  118.6 0.9 fusion.169
  119.5 5.1 %convolution_negate_fusion = f32[2,3,32,512]{3,2,1,0:T(8,128)S(1)} fusion(f32[2,3,32,512]{3,0,2,1:T(2,128)S(1)} %fusion.169), kind=kOutput, calls=%fused_computation.72 | convolution fusion | flops 607748096 | bytes 786432 | tf_op jit(solution)/shard_map/dot_general | solution.py:54
  124.6 5.1 %fusion.62 = f32[2,3,32,512]{3,2,1,0:T(8,128)S(1)} fusion(f32[2,3,32,512]{3,0,2,1:T(2,128)S(1)} %fusion.169), kind=kOutput, calls=%fused_computation.86 | convolution fusion | flops 607649792 | bytes 786432 | tf_op jit(solution)/shard_map/dot_general | solution.py:53
  129.7 0.6 fusion.110
  130.3 1.3 fusion.112
  131.6 0.6 fusion.49
  132.5 1.6 fusion.50
  135.2 2.0 collective-permute-start.8
  137.2 2.4 %collective-permute-start.9 = (f32[4,3,1024]{2,1,0:T(4,128)S(1)}, f32[4,3,1024]{2,1,0:T(4,128)S(1)}, u32[]{:S(2)}, u32[]{:S(2)}) collective-permute-start(f32[4,3,1024]{2,1,0:T(4,128)S(1)} %get-tuple-element.49), channel_id=1, source_target_pairs={{0,4},{1,5},{2,6},{3,7},{4,0},{5,1},{6,2},{7,3},{8,12},{9,13},{10,... | collective-permute-start | bytes 147464 | tf_op jit(solution)/shard_map/ppermute | solution.py:135
  139.6 1.5 collective-permute-start.11
  141.1 1.5 collective-permute-start.12
  142.6 1.1 collective-permute-start.13
  143.7 1.2 collective-permute-start.14
  145.0 2.2 %collective-permute-start.15 = (f32[4,3,1024]{2,1,0:T(4,128)S(1)}, f32[4,3,1024]{2,1,0:T(4,128)S(1)}, u32[]{:S(2)}, u32[]{:S(2)}) collective-permute-start(f32[4,3,1024]{2,1,0:T(4,128)S(1)} %get-tuple-element.43), channel_id=1, source_target_pairs={{0,10},{1,11},{2,8},{3,9},{4,14},{5,15},{6,12},{7,13},{8,2},{9,3},... | collective-permute-start | bytes 147464 | tf_op jit(solution)/shard_map/ppermute | solution.py:135
  147.1 1.7 collective-permute-start.16
  148.8 0.7 collective-permute-start.17
  149.6 3.3 %collective-permute-start.18 = (f32[4,3,1024]{2,1,0:T(4,128)S(1)}, f32[4,3,1024]{2,1,0:T(4,128)}, u32[]{:S(2)}, u32[]{:S(2)}) collective-permute-start(f32[4,3,1024]{2,1,0:T(4,128)S(1)} %get-tuple-element.40), channel_id=1, source_target_pairs={{0,13},{1,12},{2,15},{3,14},{4,9},{5,8},{6,11},{7,10},{8,5},{9,4},... | collective-permute-start | bytes 147464 | tf_op jit(solution)/shard_map/ppermute | solution.py:135
  152.9 0.8 collective-permute-done.14
  153.8 0.7 collective-permute-start.19
  154.5 0.7 collective-permute-done.15
  155.2 2.2 %collective-permute-start.20 = (f32[4,3,1024]{2,1,0:T(4,128)S(1)}, f32[4,3,1024]{2,1,0:T(4,128)}, u32[]{:S(2)}, u32[]{:S(2)}) collective-permute-start(f32[4,3,1024]{2,1,0:T(4,128)S(1)} %get-tuple-element.38), channel_id=1, source_target_pairs={{0,15},{1,14},{2,13},{3,12},{4,11},{5,10},{6,9},{7,8},{8,7},{9,6},... | collective-permute-start | bytes 147464 | tf_op jit(solution)/shard_map/ppermute | solution.py:135
  161.4 1.1 dynamic_update_slice.58
  162.5 1.1 dynamic_update_slice.59
  163.6 1.1 dynamic_update_slice.60
  164.8 1.3 collective-permute-done.18
  166.1 1.1 dynamic_update_slice.61
  167.2 1.1 dynamic_update_slice.62
  168.3 1.3 dynamic_update_slice.63
  169.7 0.6 fusion.81
  170.3 0.6 fusion.83
  171.0 0.6 fusion.51
  171.6 0.7 fusion.55
  172.3 0.6 convolution_bitcast_fusion
  172.9 0.6 convolution_bitcast_fusion.1
  173.5 1.4 copy.47
  174.9 7.1 %all-to-all-start = ((f32[4,48,1024]{2,0,1:T(4,128)}), f32[4,48,1024]{2,0,1:T(4,128)S(1)}, u32[]{:S(2)}, u32[]{:S(2)}) async-start(f32[4,48,1024]{2,0,1:T(4,128)} %copy.47), calls=%async_computation | async-start | bytes 1572864 | tf_op jit(solution)/shard_map/all_to_all | solution.py:139
  182.0 2.1 copy.50
  184.1 17.5 %all-to-all-done = f32[4,48,1024]{2,0,1:T(4,128)S(1)} async-done(((f32[4,48,1024]{2,0,1:T(4,128)}), f32[4,48,1024]{2,0,1:T(4,128)S(1)}, u32[]{:S(2)}, u32[]{:S(2)}) %all-to-all-start) | async-done | bytes 786464 | tf_op jit(solution)/shard_map/all_to_all | solution.py:139
  202.1 0.5 fusion.106
  202.9 0.5 fusion.108
  203.4 0.6 fusion.47
  204.0 0.6 fusion.48
  204.5 5.1 %fusion.60 = f32[2,3,32,512]{3,2,1,0:T(8,128)S(1)} fusion(f32[2,3,32,512]{3,2,1,0:T(8,128)S(1)} %fusion.48), kind=kOutput, calls=%fused_computation.84 | convolution fusion | flops 607649792 | bytes 786432 | tf_op jit(solution)/shard_map/dot_general | solution.py:96
  209.6 5.6 %fusion.56 = f32[2,3,32,512]{3,2,1,0:T(8,128)} fusion(f32[2,3,32,512]{3,2,1,0:T(8,128)S(1)} %fusion.60, f32[2,3,32,512]{3,2,1,0:T(8,128)S(1)} %fusion.47), kind=kOutput, calls=%fused_computation.80 | convolution fusion | flops 607846400 | bytes 1179648 | tf_op jit(solution)/shard_map/dot_general | solution.py:96
  (70 shorter events, 7.1 us)
Async XLA Ops:
  3.5 14.6 %collective-permute-start = (f32[8,1,32,512]{3,0,2,1:T(8,128)}, f32[8,1,32,512]{3,0,2,1:T(8,128)}, u32[]{:S(2)}, u32[]{:S(2)}) collective-permute-start(f32[8,1,32,512]{3,0,2,1:T(8,128)} %get-tuple-element.36), channel_id=1, source_target_pairs={{1,0},{2,1},{3,2},{4,3},{5,4},{6,5},{7,6},{8,7},{9,8},{10,9},{11,1... | collective-permute-start | bytes 1572872 | tf_op jit(solution)/shard_map/ppermute | solution.py:20
  4.2 13.9 %collective-permute-start.1 = (f32[8,1,32,512]{3,0,2,1:T(8,128)}, f32[8,1,32,512]{3,0,2,1:T(8,128)}, u32[]{:S(2)}, u32[]{:S(2)}) collective-permute-start(f32[8,1,32,512]{3,0,2,1:T(8,128)} %get-tuple-element.37), channel_id=1, source_target_pairs={{0,1},{1,2},{2,3},{3,4},{4,5},{5,6},{6,7},{7,8},{8,9},{9,10},{10,1... | collective-permute-start | bytes 1572872 | tf_op jit(solution)/shard_map/ppermute | solution.py:19
  6.9 0.9 copy-start.3
  6.9 1.4 copy-start.5
  10.2 7.9 %copy-start = (f32[8,3,31,512]{3,0,2,1:T(8,128)S(1)}, f32[8,3,31,512]{3,0,2,1:T(8,128)}, u32[]{:S(2)}) copy-start(f32[8,3,31,512]{3,0,2,1:T(8,128)} %get-tuple-element.35) | copy-start | bytes 4571140
  10.2 7.9 %copy-start.1 = (f32[8,3,32,512]{3,0,2,1:T(8,128)S(1)}, f32[8,3,32,512]{3,0,2,1:T(8,128)}, u32[]{:S(2)}) copy-start(f32[8,3,32,512]{3,0,2,1:T(8,128)} %multiply_subtract_fusion.2) | copy-start | bytes 4718596
  10.2 7.9 %copy-start.2 = (f32[8,3,32,1]{3,0,2,1:T(8,128)S(1)}, f32[8,3,32,1]{3,0,2,1:T(8,128)}, u32[]{:S(2)}) copy-start(f32[8,3,32,1]{3,0,2,1:T(8,128)} %get-tuple-element.29) | copy-start | bytes 9220
  10.2 7.9 %copy-start.4 = (s32[3,32,512]{2,1,0:T(8,128)S(1)}, s32[3,32,512]{2,1,0:T(8,128)}, u32[]{:S(2)}) copy-start(s32[3,32,512]{2,1,0:T(8,128)} %param.4) | copy-start | bytes 589828
  10.3 7.9 %copy-start.7 = (s32[8,8]{1,0:T(8,128)S(1)}, s32[8,8]{1,0:T(8,128)}, u32[]{:S(2)}) copy-start(s32[8,8]{1,0:T(8,128)} %param.6) | copy-start | bytes 772
  22.2 14.0 %collective-permute-start.2 = (f32[8,1,32,512]{3,0,2,1:T(8,128)S(1)}, f32[8,1,32,512]{3,0,2,1:T(8,128)S(1)}, u32[]{:S(2)}, u32[]{:S(2)}) collective-permute-start(f32[8,1,32,512]{3,0,2,1:T(8,128)S(1)} %get-tuple-element.26), channel_id=1, source_target_pairs={{1,0},{2,1},{3,2},{4,3},{5,4},{6,5},{7,6},{8,7},{9,8},{10,9},{11,1... | collective-permute-start | bytes 1572872 | tf_op jit(solution)/shard_map/ppermute | solution.py:20
  22.3 13.9 %collective-permute-start.3 = (f32[8,1,32,512]{3,0,2,1:T(8,128)S(1)}, f32[8,1,32,512]{3,0,2,1:T(8,128)S(1)}, u32[]{:S(2)}, u32[]{:S(2)}) collective-permute-start(f32[8,1,32,512]{3,0,2,1:T(8,128)S(1)} %get-tuple-element.27), channel_id=1, source_target_pairs={{0,1},{1,2},{2,3},{3,4},{4,5},{5,6},{6,7},{7,8},{8,9},{9,10},{10,1... | collective-permute-start | bytes 1572872 | tf_op jit(solution)/shard_map/ppermute | solution.py:19
  71.5 12.4 %collective-permute-start.4 = (f32[8,1,32,512]{3,0,2,1:T(8,128)S(1)}, f32[8,1,32,512]{3,0,2,1:T(8,128)S(1)}, u32[]{:S(2)}, u32[]{:S(2)}) collective-permute-start(f32[8,1,32,512]{3,0,2,1:T(8,128)S(1)} %get-tuple-element.16), channel_id=1, source_target_pairs={{1,0},{2,1},{3,2},{4,3},{5,4},{6,5},{7,6},{8,7},{9,8},{10,9},{11,1... | collective-permute-start | bytes 1572872 | tf_op jit(solution)/shard_map/ppermute | solution.py:20
  71.6 12.3 %collective-permute-start.5 = (f32[8,1,32,512]{3,0,2,1:T(8,128)S(1)}, f32[8,1,32,512]{3,0,2,1:T(8,128)S(1)}, u32[]{:S(2)}, u32[]{:S(2)}) collective-permute-start(f32[8,1,32,512]{3,0,2,1:T(8,128)S(1)} %get-tuple-element.17), channel_id=1, source_target_pairs={{0,1},{1,2},{2,3},{3,4},{4,5},{5,6},{6,7},{7,8},{8,9},{9,10},{10,1... | collective-permute-start | bytes 1572872 | tf_op jit(solution)/shard_map/ppermute | solution.py:19
  83.9 34.7 %copy-start.8 = (s32[2]{0:T(128)S(1)}, s32[2]{0:T(128)}, u32[]{:S(2)}) copy-start(s32[2]{0:T(128)} %param.7) | copy-start | bytes 28
  135.0 4.6 %collective-permute-start.6 = (f32[4,3,1024]{2,1,0:T(4,128)S(1)}, f32[4,3,1024]{2,1,0:T(4,128)S(1)}, u32[]{:S(2)}, u32[]{:S(2)}) collective-permute-start(f32[4,3,1024]{2,1,0:T(4,128)S(1)} %get-tuple-element.52), channel_id=1, source_target_pairs={{0,1},{1,0},{2,3},{3,2},{4,5},{5,4},{6,7},{7,6},{8,9},{9,8},{10,11... | collective-permute-start | bytes 147464 | tf_op jit(solution)/shard_map/ppermute | solution.py:135
  135.1 6.0 %collective-permute-start.7 = (f32[4,3,1024]{2,1,0:T(4,128)S(1)}, f32[4,3,1024]{2,1,0:T(4,128)S(1)}, u32[]{:S(2)}, u32[]{:S(2)}) collective-permute-start(f32[4,3,1024]{2,1,0:T(4,128)S(1)} %get-tuple-element.51), channel_id=1, source_target_pairs={{0,2},{1,3},{2,0},{3,1},{4,6},{5,7},{6,4},{7,5},{8,10},{9,11},{10,... | collective-permute-start | bytes 147464 | tf_op jit(solution)/shard_map/ppermute | solution.py:135
  135.2 7.5 %collective-permute-start.8 = (f32[4,3,1024]{2,1,0:T(4,128)S(1)}, f32[4,3,1024]{2,1,0:T(4,128)S(1)}, u32[]{:S(2)}, u32[]{:S(2)}) collective-permute-start(f32[4,3,1024]{2,1,0:T(4,128)S(1)} %get-tuple-element.50), channel_id=1, source_target_pairs={{0,3},{1,2},{2,1},{3,0},{4,7},{5,6},{6,5},{7,4},{8,11},{9,10},{10,... | collective-permute-start | bytes 147464 | tf_op jit(solution)/shard_map/ppermute | solution.py:135
  137.2 6.5 %collective-permute-start.9 = (f32[4,3,1024]{2,1,0:T(4,128)S(1)}, f32[4,3,1024]{2,1,0:T(4,128)S(1)}, u32[]{:S(2)}, u32[]{:S(2)}) collective-permute-start(f32[4,3,1024]{2,1,0:T(4,128)S(1)} %get-tuple-element.49), channel_id=1, source_target_pairs={{0,4},{1,5},{2,6},{3,7},{4,0},{5,1},{6,2},{7,3},{8,12},{9,13},{10,... | collective-permute-start | bytes 147464 | tf_op jit(solution)/shard_map/ppermute | solution.py:135
  139.6 5.4 %collective-permute-start.10 = (f32[4,3,1024]{2,1,0:T(4,128)S(1)}, f32[4,3,1024]{2,1,0:T(4,128)S(1)}, u32[]{:S(2)}, u32[]{:S(2)}) collective-permute-start(f32[4,3,1024]{2,1,0:T(4,128)S(1)} %get-tuple-element.48), channel_id=1, source_target_pairs={{0,5},{1,4},{2,7},{3,6},{4,1},{5,0},{6,3},{7,2},{8,13},{9,12},{10,... | collective-permute-start | bytes 147464 | tf_op jit(solution)/shard_map/ppermute | solution.py:135
  139.6 7.5 %collective-permute-start.11 = (f32[4,3,1024]{2,1,0:T(4,128)S(1)}, f32[4,3,1024]{2,1,0:T(4,128)S(1)}, u32[]{:S(2)}, u32[]{:S(2)}) collective-permute-start(f32[4,3,1024]{2,1,0:T(4,128)S(1)} %get-tuple-element.47), channel_id=1, source_target_pairs={{0,6},{1,7},{2,4},{3,5},{4,2},{5,3},{6,0},{7,1},{8,14},{9,15},{10,... | collective-permute-start | bytes 147464 | tf_op jit(solution)/shard_map/ppermute | solution.py:135
  141.1 7.7 %collective-permute-start.12 = (f32[4,3,1024]{2,1,0:T(4,128)S(1)}, f32[4,3,1024]{2,1,0:T(4,128)S(1)}, u32[]{:S(2)}, u32[]{:S(2)}) collective-permute-start(f32[4,3,1024]{2,1,0:T(4,128)S(1)} %get-tuple-element.46), channel_id=1, source_target_pairs={{0,7},{1,6},{2,5},{3,4},{4,3},{5,2},{6,1},{7,0},{8,15},{9,14},{10,... | collective-permute-start | bytes 147464 | tf_op jit(solution)/shard_map/ppermute | solution.py:135
  142.6 7.0 %collective-permute-start.13 = (f32[4,3,1024]{2,1,0:T(4,128)S(1)}, f32[4,3,1024]{2,1,0:T(4,128)S(1)}, u32[]{:S(2)}, u32[]{:S(2)}) collective-permute-start(f32[4,3,1024]{2,1,0:T(4,128)S(1)} %get-tuple-element.45), channel_id=1, source_target_pairs={{0,8},{1,9},{2,10},{3,11},{4,12},{5,13},{6,14},{7,15},{8,0},{9,1},... | collective-permute-start | bytes 147464 | tf_op jit(solution)/shard_map/ppermute | solution.py:135
  143.7 10.0 %collective-permute-start.14 = (f32[4,3,1024]{2,1,0:T(4,128)S(1)}, f32[4,3,1024]{2,1,0:T(4,128)S(1)}, u32[]{:S(2)}, u32[]{:S(2)}) collective-permute-start(f32[4,3,1024]{2,1,0:T(4,128)S(1)} %get-tuple-element.44), channel_id=1, source_target_pairs={{0,9},{1,8},{2,11},{3,10},{4,13},{5,12},{6,15},{7,14},{8,1},{9,0},... | collective-permute-start | bytes 147464 | tf_op jit(solution)/shard_map/ppermute | solution.py:135
  145.0 10.2 %collective-permute-start.15 = (f32[4,3,1024]{2,1,0:T(4,128)S(1)}, f32[4,3,1024]{2,1,0:T(4,128)S(1)}, u32[]{:S(2)}, u32[]{:S(2)}) collective-permute-start(f32[4,3,1024]{2,1,0:T(4,128)S(1)} %get-tuple-element.43), channel_id=1, source_target_pairs={{0,10},{1,11},{2,8},{3,9},{4,14},{5,15},{6,12},{7,13},{8,2},{9,3},... | collective-permute-start | bytes 147464 | tf_op jit(solution)/shard_map/ppermute | solution.py:135
  147.1 15.4 %collective-permute-start.16 = (f32[4,3,1024]{2,1,0:T(4,128)S(1)}, f32[4,3,1024]{2,1,0:T(4,128)}, u32[]{:S(2)}, u32[]{:S(2)}) collective-permute-start(f32[4,3,1024]{2,1,0:T(4,128)S(1)} %get-tuple-element.42), channel_id=1, source_target_pairs={{0,11},{1,10},{2,9},{3,8},{4,15},{5,14},{6,13},{7,12},{8,3},{9,2},... | collective-permute-start | bytes 147464 | tf_op jit(solution)/shard_map/ppermute | solution.py:135
  148.8 14.8 %collective-permute-start.17 = (f32[4,3,1024]{2,1,0:T(4,128)S(1)}, f32[4,3,1024]{2,1,0:T(4,128)}, u32[]{:S(2)}, u32[]{:S(2)}) collective-permute-start(f32[4,3,1024]{2,1,0:T(4,128)S(1)} %get-tuple-element.41), channel_id=1, source_target_pairs={{0,12},{1,13},{2,14},{3,15},{4,8},{5,9},{6,10},{7,11},{8,4},{9,5},... | collective-permute-start | bytes 147464 | tf_op jit(solution)/shard_map/ppermute | solution.py:135
  149.6 16.5 %collective-permute-start.18 = (f32[4,3,1024]{2,1,0:T(4,128)S(1)}, f32[4,3,1024]{2,1,0:T(4,128)}, u32[]{:S(2)}, u32[]{:S(2)}) collective-permute-start(f32[4,3,1024]{2,1,0:T(4,128)S(1)} %get-tuple-element.40), channel_id=1, source_target_pairs={{0,13},{1,12},{2,15},{3,14},{4,9},{5,8},{6,11},{7,10},{8,5},{9,4},... | collective-permute-start | bytes 147464 | tf_op jit(solution)/shard_map/ppermute | solution.py:135
  153.8 13.4 %collective-permute-start.19 = (f32[4,3,1024]{2,1,0:T(4,128)S(1)}, f32[4,3,1024]{2,1,0:T(4,128)}, u32[]{:S(2)}, u32[]{:S(2)}) collective-permute-start(f32[4,3,1024]{2,1,0:T(4,128)S(1)} %get-tuple-element.39), channel_id=1, source_target_pairs={{0,14},{1,15},{2,12},{3,13},{4,10},{5,11},{6,8},{7,9},{8,6},{9,7},... | collective-permute-start | bytes 147464 | tf_op jit(solution)/shard_map/ppermute | solution.py:135
  155.2 2.2 %copy-start.6 = (f32[4,3,1024]{2,1,0:T(4,128)}, f32[4,3,1024]{2,1,0:T(4,128)S(1)}, u32[]{:S(2)}) copy-start(f32[4,3,1024]{2,1,0:T(4,128)S(1)} %collective-permute-done.15) | copy-start | bytes 147460
  155.2 13.2 %collective-permute-start.20 = (f32[4,3,1024]{2,1,0:T(4,128)S(1)}, f32[4,3,1024]{2,1,0:T(4,128)}, u32[]{:S(2)}, u32[]{:S(2)}) collective-permute-start(f32[4,3,1024]{2,1,0:T(4,128)S(1)} %get-tuple-element.38), channel_id=1, source_target_pairs={{0,15},{1,14},{2,13},{3,12},{4,11},{5,10},{6,9},{7,8},{8,7},{9,6},... | collective-permute-start | bytes 147464 | tf_op jit(solution)/shard_map/ppermute | solution.py:135
  174.9 26.7 %all-to-all-start = ((f32[4,48,1024]{2,0,1:T(4,128)}), f32[4,48,1024]{2,0,1:T(4,128)S(1)}, u32[]{:S(2)}, u32[]{:S(2)}) async-start(f32[4,48,1024]{2,0,1:T(4,128)} %copy.47), calls=%async_computation | async-start | bytes 1572864 | tf_op jit(solution)/shard_map/all_to_all | solution.py:139
